TPU v7x, 256 devices: a whole 4x4x8 slice. The times are simulated.
256 devices in a mesh: dp: 8 (over x_hi, y), tensor: 32 (over z, x_lo, core).
Axes of the slice: x: 4 (x_hi: 2, x_lo: 2; x = x_hi * 2 + x_lo), y: 4, z: 8, core: 2. Of those that a mesh axis runs over, the one named last changes fastest.
Arguments:
- hidden: bfloat16 [4096, 16384], P('dp', 'tensor'), may hold values from -6 to 6
- down_weight: bfloat16 [16384, 8192], P('tensor'), may hold values from -0.046875 to 0.046875
- adapter_first_factor: bfloat16 [16384, 1024], P('tensor'), may hold values from -0.046875 to 0.046875
- adapter_second_factor: bfloat16 [1024, 8192], P(None, 'tensor'), may hold values from -1.5 to 1.5
- output_gradient: bfloat16 [4096, 8192], P(('dp', 'tensor')), may hold values from -6 to 6
- token_language_index: int32 [8, 512], P('dp'), may hold values from 0 to 63, never falling along the last dimension, each value on 1 to 128 neighbouring positions
- owned: int32 [64], replicated, may hold values from 0 to 63, each once
Outputs:
- mixed: bfloat16 [4096, 8192], P(('dp', 'tensor'))
- hidden_gradient: bfloat16 [4096, 16384], P('dp', 'tensor')
- grad_a: float32 [64, 16, 16384], P('dp', None, 'tensor')
- grad_b: float32 [64, 16, 8192], P('dp', None, 'tensor')
Inputs may be any that keep to these rules, and one draw needn't show every extreme that they name: Each row of token_language_index never falls and names every language; one language has exactly 128 tokens of the row, none more. `owned`: each adapter appears once.
All inputs are finite; a program needn't handle non-finite values.
Results may differ from a plain program's by a relative error of at most 0.0075.
Values may be sent and summed in bfloat16 or wider, within the bound.
A program may use at most 128 MiB of HBM per device.

v0:
```python
import jax
import jax.numpy as jnp
from jax import lax
from jax.sharding import PartitionSpec as P

ADAPTER_RANK = 16
LANGUAGE_COUNT = 64


adapter_scale = 0.5


def select_language_rank(full, language_mask):
    rows = full.shape[0]
    return jnp.sum(
        full.reshape(rows, LANGUAGE_COUNT, ADAPTER_RANK) * language_mask[:, :, None], axis=1
    )


def spread_rank(small, onehot_half):
    rows = small.shape[0]
    return (onehot_half[:, :, None] * small.astype(jnp.bfloat16)[:, None, :]).reshape(
        rows, LANGUAGE_COUNT * ADAPTER_RANK
    )


def contract_matrices(left, right, left_dim, right_dim):
    return lax.dot_general(
        left, right, (((left_dim,), (right_dim,)), ((), ())), preferred_element_type=jnp.float32
    )


def body(
    hidden,
    down_weight,
    adapter_first_factor,
    adapter_second_factor,
    output_gradient,
    token_language_index,
    owned,
):
    column_share = adapter_second_factor.shape[1]
    col_start = lax.axis_index("tensor") * column_share
    labels = token_language_index.reshape(-1)
    language_mask = (
        labels[:, None] == jnp.arange(LANGUAGE_COUNT, dtype=jnp.int32)[None, :]
    ).astype(jnp.float32)
    onehot_half = language_mask.astype(jnp.bfloat16)
    gathered = lax.all_gather(output_gradient, "tensor", axis=0, tiled=True)
    gradient_column_block = lax.dynamic_slice_in_dim(gathered, col_start, column_share, 1)
    frozen_input_gradient = contract_matrices(gathered, down_weight, 1, 1)
    rank_reduce_share = select_language_rank(
        jnp.dot(hidden, adapter_first_factor, preferred_element_type=jnp.float32), language_mask
    )
    input_gradient_share = select_language_rank(
        contract_matrices(gradient_column_block, adapter_second_factor, 1, 1), language_mask
    )
    rank_reduce, input_gradient = lax.psum((rank_reduce_share, input_gradient_share), "tensor")
    expanded_rank = spread_rank(rank_reduce, onehot_half)
    gradient_spread_rank = spread_rank(input_gradient, onehot_half)
    rank_expand = adapter_scale * jnp.dot(
        expanded_rank, adapter_second_factor, preferred_element_type=jnp.float32
    )
    base_rows = lax.psum_scatter(
        jnp.dot(hidden, down_weight, preferred_element_type=jnp.float32),
        "tensor",
        scatter_dimension=0,
        tiled=True,
    )
    lift_rows = lax.all_to_all(rank_expand, "tensor", split_axis=0, concat_axis=1, tiled=True)
    mixed = (base_rows + lift_rows).astype(jnp.bfloat16)
    hidden_gradient = (
        frozen_input_gradient
        + adapter_scale * contract_matrices(gradient_spread_rank, adapter_first_factor, 1, 1)
    ).astype(jnp.bfloat16)
    resident_first_factor = adapter_scale * contract_matrices(gradient_spread_rank, hidden, 0, 0)
    resident_second_factor = adapter_scale * contract_matrices(
        expanded_rank, gradient_column_block, 0, 0
    )
    ordered_a = jnp.take(
        resident_first_factor.reshape(LANGUAGE_COUNT, ADAPTER_RANK, -1), owned, axis=0
    )
    ordered_b = jnp.take(
        resident_second_factor.reshape(LANGUAGE_COUNT, ADAPTER_RANK, -1), owned, axis=0
    )
    grad_a, grad_b = (
        lax.psum_scatter(ordered_a, "dp", scatter_dimension=0, tiled=True),
        lax.psum_scatter(ordered_b, "dp", scatter_dimension=0, tiled=True),
    )
    return (mixed, hidden_gradient, grad_a, grad_b)


def solution(mesh):
    in_specs = (
        P("dp", "tensor"),
        P("tensor", None),
        P("tensor", None),
        P(None, "tensor"),
        P(("dp", "tensor"), None),
        P("dp", None),
        P(),
    )
    out_specs = (
        P(("dp", "tensor"), None),
        P("dp", "tensor"),
        P("dp", None, "tensor"),
        P("dp", None, "tensor"),
    )
    return jax.shard_map(body, mesh=mesh, in_specs=in_specs, out_specs=out_specs, check_vma=False)
```

profile of v0, /device:TPU:32, one launch (start us, length us, event | category | flops | bytes accessed | tf_op | source)
XLA Modules:
  0.0 457.7 jit_solution(10031234196702321765)
XLA Ops:
  7.2 0.0 copy-start
  7.2 0.0 all-gather.2.cloned.1.call-start
  7.2 0.7 all-gather.2.cloned.1.call-update
  7.9 0.0 reduce-scatter.4.cloned.1.call-start
  8.0 13.8 %fusion.9 = f32[512,8192]{1,0:T(8,128)} fusion(bf16[512,512]{1,0:T(8,128)(2,1)} %param.7, bf16[512,8192]{1,0:T(8,128)(2,1)} %param.8), kind=kOutput, calls=%fused_computation.26 | convolution fusion | flops 4294967296 | bytes 25690112 | tf_op jit(solution)/shard_map/dot_general | solution.py:65
  21.8 0.0 copy-start.10
  21.8 0.0 copy-start.9
  21.8 0.0 reduce-scatter.4.cloned.1.call-update
  21.8 0.0 copy-start.7
  21.8 0.0 reduce-scatter.8.cloned.1.call-start
  21.9 0.6 copy-done.10
  22.5 0.0 copy-done.9
  22.5 0.0 copy-done
  22.5 0.3 copy-done.1
  22.9 2.1 fusion.10
  25.0 59.6 %all-gather.2.cloned.1.call-done = bf16[512,8192]{1,0:T(8,128)(2,1)} async-done(((bf16[16,8192]{1,0:T(8,128)(2,1)}), bf16[512,8192]{1,0:T(8,128)(2,1)}) %all-gather.2.cloned.1.call-update) | async-done | bytes 8388624 | tf_op jit(solution)/shard_map/all_gather | solution.py:49
  84.6 0.0 copy-done.7
  84.6 1.6 fusion.3
  86.1 0.1 copy-done.2
  86.2 0.7 multiply_reduce_fusion
  86.9 102.4 %all-reduce = (bf16[512,16]{0,1:T(8,128)(2,1)S(1)}, bf16[512,16]{0,1:T(8,128)(2,1)S(1)}) all-reduce(f32[512,16]{0,1:T(8,128)S(1)} %get-tuple-element.5, f32[512,16]{0,1:T(8,128)S(1)} %get-tuple-element.4), channel_id=1, replica_groups=mesh['dp'=8,'tensor'=32] {'tensor'}, use_global_device_ids=true, to_apply=%region_2.0 | all-reduce | flops 16384 | bytes 98304 | tf_op jit(solution)/shard_map/psum | solution.py:58
  189.3 0.1 broadcast_multiply_fusion
  189.4 0.0 copy-start.5
  189.5 0.0 copy-start.3
  189.5 1.0 copy-done.5
  190.4 2.5 convolution_multiply_fusion.2
  192.9 2.9 gather_fusion.1
  195.8 2.4 broadcast_select_fusion.1
  198.2 0.0 reduce-scatter.8.cloned.1.call-update
  198.3 0.0 reduce-scatter.6.cloned.1.call-start
  198.3 0.0 copy-done.3
  198.3 2.1 convolution_multiply_fusion
  200.4 2.3 gather_fusion
  202.7 1.6 broadcast_select_fusion
  204.3 0.0 reduce-scatter.6.cloned.1.call-update
  204.3 1.2 copy-done.6
  205.5 0.1 copy-done.8
  205.6 1.3 convolution_multiply_fusion.3
  206.9 12.0 %all-to-all-start = ((f32[32,16,256]{2,1,0:T(8,128)}), f32[32,16,256]{2,1,0:T(8,128)S(1)}, u32[]{:S(2)}, u32[]{:S(2)}) async-start(f32[32,16,256]{2,1,0:T(8,128)} %bitcast.3), calls=%async_computation.1 | async-start | bytes 1048576 | tf_op jit(solution)/shard_map/all_to_all | solution.py:70
  218.9 0.0 copy-start.4
  218.9 9.7 %fusion.11 = f32[512,512]{1,0:T(8,128)S(1)} fusion(bf16[512,8192]{1,0:T(8,128)(2,1)} %all-gather.2.cloned.1.call-done, bf16[512,8192]{1,0:T(8,128)(2,1)} %param.8), kind=kOutput, calls=%fused_computation.28 | convolution fusion | flops 4294967296 | bytes 17825792 | tf_op jit(solution)/shard_map/dot_general | solution.py:28
  228.6 0.0 copy-done.4
  228.7 1.6 fusion.1
  230.2 8.5 %all-to-all-done = f32[32,16,256]{2,1,0:T(8,128)S(1)} async-done(((f32[32,16,256]{2,1,0:T(8,128)}), f32[32,16,256]{2,1,0:T(8,128)S(1)}, u32[]{:S(2)}, u32[]{:S(2)}) %all-to-all-start) | async-done | bytes 524320 | tf_op jit(solution)/shard_map/all_to_all | solution.py:70
  238.7 43.1 %reduce-scatter.4.cloned.1.call-done = f32[16,8192]{1,0:T(8,128)} async-done(((f32[512,8192]{1,0:T(8,128)}), f32[16,8192]{1,0:T(8,128)}) %reduce-scatter.4.cloned.1.call-update) | async-done | bytes 524304 | tf_op jit(solution)/shard_map/reduce_scatter | solution.py:64
  281.8 1.8 add_convert_fusion
  283.6 83.4 %reduce-scatter.8.cloned.1.call-done = f32[8,16,256]{2,1,0:T(8,128)} async-done(((f32[64,16,256]{2,1,0:T(8,128)}), f32[8,16,256]{2,1,0:T(8,128)}) %reduce-scatter.8.cloned.1.call-update) | async-done | bytes 131088 | tf_op jit(solution)/shard_map/reduce_scatter | solution.py:88
  367.0 84.2 %reduce-scatter.6.cloned.1.call-done = f32[8,16,512]{2,1,0:T(8,128)} async-done(((f32[64,16,512]{2,1,0:T(8,128)}), f32[8,16,512]{2,1,0:T(8,128)}) %reduce-scatter.6.cloned.1.call-update) | async-done | bytes 262160 | tf_op jit(solution)/shard_map/reduce_scatter | solution.py:87
  (9 shorter events, 0.1 us)
Async XLA Ops:
  7.2 15.4 %copy-start = (bf16[512,1024]{1,0:T(8,128)(2,1)S(1)}, bf16[512,1024]{1,0:T(8,128)(2,1)}, u32[]{:S(2)}) copy-start(bf16[512,1024]{1,0:T(8,128)(2,1)} %param.9) | copy-start | bytes 3145732
  7.2 77.4 %all-gather.2.cloned.1.call-start = ((), (), s32[]{:S(2)}) async-start(), calls=%async_computation.5 | async-start | bytes 8650752 | tf_op jit(solution)/shard_map/all_gather | solution.py:49
  7.9 273.9 %reduce-scatter.4.cloned.1.call-start = ((), (), s32[]{:S(2)}) async-start(), calls=%async_computation.4 | async-start | bytes 17301504 | tf_op jit(solution)/shard_map/reduce_scatter | solution.py:64
  21.8 0.7 copy-start.10
  21.8 0.7 copy-start.9
  21.8 1.1 copy-start.1
  21.8 62.7 %copy-start.7 = (bf16[1024,256]{1,0:T(8,128)(2,1)S(1)}, bf16[1024,256]{1,0:T(8,128)(2,1)}, u32[]{:S(2)}) copy-start(bf16[1024,256]{1,0:T(8,128)(2,1)} %param.10) | copy-start | bytes 1572868
  21.8 345.2 %reduce-scatter.8.cloned.1.call-start = ((), (), s32[]{:S(2)}) async-start(), calls=%async_computation.7 | async-start | bytes 1179648 | tf_op jit(solution)/shard_map/reduce_scatter | solution.py:88
  84.6 1.7 copy-start.2
  189.4 1.0 copy-start.5
  189.5 8.9 %copy-start.3 = (bf16[512,64,16]{0,2,1:T(8,128)(2,1)}, bf16[512,64,16]{0,2,1:T(8,128)(2,1)S(1)}, u32[]{:S(2)}) copy-start(bf16[512,64,16]{0,2,1:T(8,128)(2,1)S(1)} %get-tuple-element.8) | copy-start | bytes 3145732
  198.3 252.9 %reduce-scatter.6.cloned.1.call-start = ((), (), s32[]{:S(2)}) async-start(), calls=%async_computation.6 | async-start | bytes 2359296 | tf_op jit(solution)/shard_map/reduce_scatter | solution.py:87
  204.3 1.2 copy-start.6
  204.3 1.4 copy-start.8
  206.9 31.8 %all-to-all-start = ((f32[32,16,256]{2,1,0:T(8,128)}), f32[32,16,256]{2,1,0:T(8,128)S(1)}, u32[]{:S(2)}, u32[]{:S(2)}) async-start(f32[32,16,256]{2,1,0:T(8,128)} %bitcast.3), calls=%async_computation.1 | async-start | bytes 1048576 | tf_op jit(solution)/shard_map/all_to_all | solution.py:70
  218.9 9.8 %copy-start.4 = (bf16[512,64,16]{0,2,1:T(8,128)(2,1)S(1)}, bf16[512,64,16]{0,2,1:T(8,128)(2,1)}, u32[]{:S(2)}) copy-start(bf16[512,64,16]{0,2,1:T(8,128)(2,1)} %copy-done.3) | copy-start | bytes 3145732
Sparse Core Ops, SparseCore 0:
  9.9 74.6 all-gather.1
  87.1 194.6 reduce-scatter.3
  286.3 80.6 reduce-scatter.7
  372.0 79.1 reduce-scatter.5
where the time goes:
time: 458 us
  waiting for transfers between devices  279 us (61%)
  blocking collectives  102 us (22%)
  matrix products  34.6 us (8%)
  between operations  13.9 us (3%)
  starting transfers between devices  12.1 us (3%)
  local copies, waits for them, and re-layouts  8.59 us (2%)
  other arithmetic  6.66 us (1%)
    psum x1, blocking collectives, body(): lax.psum((rank_reduce_share, input_gradient_share), 'tensor')  102 us
    reduce_scatter x1, waiting for transfers between devices, body(): lax.psum_scatter(ordered_a, 'dp', scatter_dimension=0, tiled=True)  84.2 us
    reduce_scatter x1, waiting for transfers between devices, body(): lax.psum_scatter(ordered_b, 'dp', scatter_dimension=0, tiled=True)  83.4 us
    all_gather x1, waiting for transfers between devices, body(): gathered = lax.all_gather(output_gradient, 'tensor', axis=0, tiled=True)  59.6 us
    reduce_scatter x1, waiting for transfers between devices, body(): lax.psum_scatter(jnp.dot(hidden, down_weight, preferred_element_type=jnp....  43.1 us
    dot_general x5, matrix products, contract_matrices(): lax.dot_general(left, right, (((left_dim,), (right_dim,)), ((), ())), pre...  17.4 us
    dot_general x1, matrix products, body(): jnp.dot(hidden, down_weight, preferred_element_type=jnp.float32)  13.8 us
    all_to_all x1, starting transfers between devices, body(): lax.all_to_all(rank_expand, 'tensor', split_axis=0, concat_axis=1, tiled=...  12 us
  transfers between devices with their start and end apart: 5, of which 5 were waited for; matrix products, arithmetic and copies ran while one was open for 10% of the time, Pallas kernels for 0%

commit v1 on v0

v1 whole, which is shorter than its diff:
```python
import functools

import jax
import jax.numpy as jnp
from jax import lax
from jax.experimental import pallas as pl
from jax.experimental.pallas import tpu as pltpu
from jax.sharding import PartitionSpec as P

RANK = 16
LANGS = 64
WIDE = RANK * LANGS
LANES = 128
SCALE = 0.5
MESH = pl.DeviceIdType.MESH
BF16, F32 = jnp.bfloat16, jnp.float32


def nn(a, b):
    return jnp.dot(a, b, preferred_element_type=F32)


def nt(a, b):
    return lax.dot_general(a, b, (((1,), (1,)), ((), ())), preferred_element_type=F32)


def sizes_of(mesh, hidden, grad):
    nt_, ndp = mesh.shape["tensor"], mesh.shape["dp"]
    blocks = nt_ // 2
    features = grad.shape[1]
    return dict(
        nz=nt_ // 4,
        ny=ndp // 2,
        ndp=ndp,
        blocks=blocks,
        block=features // nt_,
        half=features // 2,
        rows=grad.shape[0],
        tokens=hidden.shape[0],
        units=hidden.shape[1],
        early=blocks * 7 // 16,
    )


def kernel(
    sz,
    hidden_ref, weight_ref, first_ref, second_ref, grad_ref, lab_col, lab_row, own_ref,
    mixed_out, hg_out, ga_out, gb_out,
    wk, hk, av, bv, gall, part, zr_p, zr_q, xr_q, xr_p, stage, mixbuf,
    ar_own, ar_quad, ar_z, ar_fin, sp_nat, sp_t, bk_nat, bk_t, lift,
    hg_own, hg_send, hg_recv, gb_part, ga_part, yr_b, yr_a, xs_b, xs_a, xr_b, xr_a,
    load_sem, swap_send, swap_recv,
    agz_s, agz_r, agp_s, agp_r, agq_s, agq_r,
    rsz_s, rsz_r, rsq_s, rsq_r, rsp_s, rsp_r, mix_s, mix_r,
    arq_s, arq_r, arz_s, arz_r, arf_s, arf_r,
    y_s, y_r, xh_s, xh_r, hg_s, hg_r,
):
    nz, ny, nb, fb, fh = sz["nz"], sz["ny"], sz["blocks"], sz["block"], sz["half"]
    rows, tokens, units = sz["rows"], sz["tokens"], sz["units"]
    quarter = tokens // 4
    own_rows = WIDE // sz["ndp"]
    pw = sz["early"] * fb
    pcols, qcols = slice(0, pw), slice(pw, fh)

    d, t = lax.axis_index("dp"), lax.axis_index("tensor")
    c, x, z, u = t % 2, (t // 2) % 2, t // 4, t % 4
    y, h = d % ny, d // ny
    jown = 2 * z + x

    core_dev = (d, t + 1 - 2 * c)
    x_dev = (d, t + 2 - 4 * x)
    quad_u = {1: u + 1 - 2 * c, 2: u + 2 - 4 * x, 3: 3 - u}

    def zwrap(v):
        return (v + 2 * nz) % nz

    def z_dev(k):
        return (d, zwrap(z + k) * 4 + u)

    def quad_dev(k):
        return (d, z * 4 + quad_u[k])

    def y_dev(k):
        return (h * ny + (y + k) % ny, t)

    h_dev = ((1 - h) * ny + y, t)

    def remote(src, dst, ssem, rsem, dev):
        return pltpu.make_async_remote_copy(
            src_ref=src, dst_ref=dst, send_sem=ssem, recv_sem=rsem, device_id=dev, device_id_type=MESH
        )

    def aligned(v, m):
        return pl.multiple_of(v, m)

    def slab(ref, zs, xs, cs, cols):
        return ref.at[pl.ds(aligned((zs * 4 + xs * 2 + cs) * rows, rows), rows), cols]

    def feat(j):
        return pl.ds(aligned(j * fb, fb), fb)

    def unit(k):
        return pl.ds(aligned(k * units, units), units)

    peers = [quad_dev(k) for k in (1, 2, 3)] + [z_dev(k) for k in range(1, nz)]
    peers += [y_dev(k) for k in range(1, ny)] + [h_dev]
    barrier = pltpu.get_barrier_semaphore()
    for peer in peers:
        pl.semaphore_signal(barrier, inc=1, device_id=peer, device_id_type=MESH)

    whole = slice(None)
    for j in range(nb):
        pltpu.make_async_copy(
            grad_ref.at[:, feat(2 * j + c)], slab(gall, z, x, c, pl.ds(j * fb, fb)), load_sem.at[0]
        ).start()
    load_h = pltpu.make_async_copy(hidden_ref, hk.at[:, unit(c)], load_sem.at[1])
    load_a = pltpu.make_async_copy(first_ref, av, load_sem.at[2])
    load_b = pltpu.make_async_copy(second_ref, bv, load_sem.at[3])
    load_h.start()
    load_a.start()
    pl.semaphore_wait(barrier, len(peers))

    for j in range(nb):
        remote(
            grad_ref.at[:, feat(2 * j + 1 - c)], slab(gall, z, x, c, pl.ds(j * fb, fb)),
            swap_send.at[0], swap_recv.at[0], core_dev,
        ).start()
    remote(hidden_ref, hk.at[:, unit(c)], swap_send.at[1], swap_recv.at[1], core_dev).start()
    for j in range(nb):
        pltpu.make_async_copy(
            weight_ref.at[:, feat(2 * j + c)], wk.at[unit(c), pl.ds(j * fb, fb)], load_sem.at[4]
        ).start()
        remote(
            weight_ref.at[:, feat(2 * j + 1 - c)], wk.at[unit(c), pl.ds(j * fb, fb)],
            swap_send.at[2], swap_recv.at[2], core_dev,
        ).start()
    load_b.start()

    def swap_wait(i):
        region = {
            0: lambda k: slab(gall, z, x, k, whole),
            1: lambda k: hk.at[:, unit(k)],
            2: lambda k: wk.at[unit(k), :],
        }[i]
        mine, theirs = region(c), region(1 - c)
        return (
            remote(theirs, theirs, swap_send.at[i], swap_recv.at[i], core_dev),
            remote(mine, mine, swap_send.at[i], swap_recv.at[i], core_dev),
        )

    def sign(way):
        return 1 - 2 * way

    chain_cols = (pcols, pcols, qcols)

    def chain_x(chain):
        return 1 - x if chain == 1 else x

    def ag_z(way, chain, s):
        ref = slab(gall, zwrap(z - sign(way) * s), chain_x(chain), way, chain_cols[chain])
        return remote(ref, ref, agz_s.at[way, chain, s], agz_r.at[way, chain, s], z_dev(sign(way)))

    def ag_z_in(way, chain, s):
        ref = slab(gall, zwrap(z - sign(way) * (s + 1)), chain_x(chain), way, chain_cols[chain])
        return remote(ref, ref, agz_s.at[way, chain, s], agz_r.at[way, chain, s], z_dev(sign(way)))

    def ag_p(way, xs):
        ref = slab(gall, z, xs, way, pcols)
        return remote(ref, ref, agp_s.at[way], agp_r.at[way], x_dev)

    def ag_q(way, k, xs):
        ref = slab(gall, zwrap(z - sign(way) * k), xs, way, qcols)
        return remote(ref, ref, agq_s.at[way, k], agq_r.at[way, k], x_dev)

    pltpu.make_async_copy(
        slab(gall, z, x, c, whole), slab(gall, z, x, c, whole), load_sem.at[0]
    ).wait()
    swap_wait(0)[0].wait_recv()
    for way in (0, 1):
        ag_p(way, x).start()
        ag_z(way, 0, 0).start()
        ag_z(way, 2, 0).start()
    for way in (0, 1):
        ag_q(way, 0, x).start()
    for way in (0, 1):
        ag_p(way, 1 - x).wait_recv()
        ag_z(way, 1, 0).start()

    def ag_step(s):
        for chain in (0, 2, 1):
            for way in (0, 1):
                ag_z_in(way, chain, s).wait_recv()
                if s + 1 < nz - 1:
                    ag_z(way, chain, s + 1).start()
                if chain == 2:
                    ag_q(way, s + 1, x).start()

    lane_lang = lax.broadcasted_iota(jnp.int32, (tokens, LANES), 1) // RANK
    per = LANES // RANK

    def pick(product, i):
        labels = jnp.broadcast_to(lab_col[...], (tokens, LANES))
        total = jnp.zeros((tokens, LANES), F32)
        step = 2 * LANES
        for g in range(WIDE // step):
            full = product(g * step, step)
            for k in range(2):
                lang = lane_lang + (2 * g + k) * per
                total += jnp.where(labels == lang, full[:, k * LANES : (k + 1) * LANES], 0.0)
        turned = total.T
        small = turned[:RANK]
        for g in range(1, per):
            small += turned[g * RANK : (g + 1) * RANK]
        for k in range(4):
            ar_own[i, k] = small[:, k * quarter : (k + 1) * quarter]

    def arq(i, k):
        return remote(ar_own.at[i, quad_u[k]], ar_quad.at[i, u], arq_s.at[i, k - 1], arq_r.at[i, k - 1], quad_dev(k))

    def arq_in(i, k):
        ref = ar_quad.at[i, quad_u[k]]
        return remote(ref, ref, arq_s.at[i, k - 1], arq_r.at[i, k - 1], quad_dev(k))

    def arz(i, k):
        ref = ar_z.at[i, z]
        return remote(ref, ref, arz_s.at[i, k - 1], arz_r.at[i, k - 1], z_dev(k))

    def arz_in(i, k):
        ref = ar_z.at[i, zwrap(z - k)]
        return remote(ref, ref, arz_s.at[i, k - 1], arz_r.at[i, k - 1], z_dev(k))

    def arf(i, k):
        ref = ar_fin.at[i, u]
        return remote(ref, ref, arf_s.at[i, k - 1], arf_r.at[i, k - 1], quad_dev(k))

    def arf_in(i, k):
        ref = ar_fin.at[i, quad_u[k]]
        return remote(ref, ref, arf_s.at[i, k - 1], arf_r.at[i, k - 1], quad_dev(k))

    def ar_first(i):
        for k in (3, 2, 1):
            arq(i, k).start()

    def ar_second(i):
        for k in (1, 2, 3):
            arq_in(i, k).wait_recv()
        total = ar_own[i, u]
        for k in (1, 2, 3):
            total += ar_quad[i, quad_u[k]]
        ar_z[i, z] = total
        for k in range(nz - 1, 0, -1):
            arz(i, k).start()

    def ar_third(i):
        for k in range(1, nz):
            arz_in(i, k).wait_recv()
        total = ar_z[i, 0]
        for k in range(1, nz):
            total += ar_z[i, k]
        ar_fin[i, u] = total
        for k in (3, 2, 1):
            arf(i, k).start()

    def ar_last(i, natural, turned):
        for k in (1, 2, 3):
            arf_in(i, k).wait_recv()
        small = jnp.concatenate([ar_fin[i, k] for k in range(4)], axis=1)
        languages = lab_row[...]
        for k in range(LANGS):
            turned[k * RANK : (k + 1) * RANK, :] = jnp.where(languages == own_ref[k], small, 0.0).astype(BF16)
        tall = jnp.concatenate([small] * per, axis=0).T
        labels = jnp.broadcast_to(lab_col[...], (tokens, LANES))
        for g in range(WIDE // LANES):
            natural[:, g * LANES : (g + 1) * LANES] = jnp.where(
                labels == lane_lang + g * per, tall, 0.0
            ).astype(BF16)

    def mix_blocks(lo, hi):
        def one(i, carry):
            cols = feat((jown + 1 + i) % nb)
            part[:, cols] = nn(hk[...], wk[:, cols]).astype(BF16)
            return carry

        if hi > lo:
            lax.fori_loop(lo, hi, one, 0)

    def mix_own():
        cols = feat(jown)
        part[:, cols] = (nn(hk[...], wk[:, cols]) + lift[...]).astype(BF16)

    load_h.wait()
    load_a.wait()
    h_own = hk[:, unit(c)]
    pick(lambda lo, n: nn(h_own, av[:, lo : lo + n]), 0)
    ar_first(0)

    splits = [(nb - 1) * s // (nz - 1) for s in range(nz)]
    for s in range(nz - 1):
        ag_step(s)
        if s == 0:
            ar_second(0)
            swap_wait(1)[0].wait_recv()
            swap_wait(2)[0].wait_recv()
            pltpu.make_async_copy(wk.at[unit(c), :], wk.at[unit(c), :], load_sem.at[4]).wait()
        if s == min(2, nz - 2):
            ar_third(0)
        if s == min(3, nz - 2):
            load_b.wait()
            ar_last(0, sp_nat, sp_t)
            lift[...] = SCALE * nn(sp_nat[...], bv[...])
        mix_blocks(splits[s], splits[s + 1])
    mix_own()

    def rs_z(way, chain, s):
        src = slab(part, zwrap(z - sign(way) * (s + 1)), chain_x(chain), way, chain_cols[chain])
        dst = zr_q.at[way, s] if chain == 2 else zr_p.at[way, s, chain]
        return remote(src, dst, rsz_s.at[way, chain, s], rsz_r.at[way, chain, s], z_dev(sign(way)))

    def rs_q(way, k):
        zs = zwrap(z - sign(way) * (k + 1))
        src = slab(part, zs, 1 - x, way, qcols)
        return remote(src, xr_q.at[zs, way], rsq_s.at[way, k], rsq_r.at[way, k], x_dev)

    def rs_p(way):
        src = slab(part, z, 1 - x, way, pcols)
        return remote(src, xr_p.at[way], rsp_s.at[way], rsp_r.at[way], x_dev)

    def rs_sum(way, chain, s):
        zs = zwrap(z - sign(way) * (s + 1))
        total = slab(part, zs, chain_x(chain), way, chain_cols[chain])[...].astype(F32)
        if chain == 2:
            rs_q(way, s).wait_recv()
            total += xr_q[zs, way].astype(F32)
        if s > 0:
            rs_z(way, chain, s - 1).wait_recv()
            got = zr_q[way, s - 1] if chain == 2 else zr_p[way, s - 1, chain]
            total += got.astype(F32)
        return total

    def rs_step(s):
        for chain in (1, 2, 0):
            for way in (0, 1):
                if s > 0 or chain == 2:
                    zs = zwrap(z - sign(way) * (s + 1))
                    slab(part, zs, chain_x(chain), way, chain_cols[chain])[...] = rs_sum(way, chain, s).astype(BF16)
                rs_z(way, chain, s).start()

    tile = min(256, units)
    mtile = tokens // 2
    ntiles = units // tile

    def hg_send_copy():
        return remote(hg_send, hg_recv, hg_s, hg_r, core_dev)

    def hg_piece(i):
        part_of, rest = i // (2 * ntiles), i % (2 * ntiles)
        n, m = rest // 2, rest % 2
        owner = c if part_of else 1 - c
        rows_of = pl.ds(aligned(owner * units + n * tile, tile), tile)
        value = nt(gall[m * mtile : (m + 1) * mtile, :], wk[rows_of, :])
        place = (slice(m * mtile, (m + 1) * mtile), slice(n * tile, (n + 1) * tile))
        if part_of:
            hg_own[place] = value
        else:
            hg_send[place] = value.astype(BF16)
        if i == 2 * ntiles - 1:
            hg_send_copy().start()

    pieces = list(range(4 * ntiles))

    def hg_some(count):
        for _ in range(min(count, len(pieces))):
            hg_piece(pieces.pop(0))

    def grads(turned, right, out):
        step = 256

        def one(i, carry):
            at = pl.ds(aligned(i * step, step), step)
            out[at, :] = (SCALE * nn(turned[at, :], right)).astype(BF16)
            return carry

        lax.fori_loop(0, WIDE // step, one, 0)

    sets = ((gb_part, yr_b, xs_b, xr_b, gb_out), (ga_part, yr_a, xs_a, xr_a, ga_out))

    def owner_rows(ref, hh, yy):
        return ref.at[pl.ds(aligned((hh * ny + yy) * own_rows, own_rows), own_rows), :]

    def y_copy(i, k, hh):
        src = owner_rows(sets[i][0], hh, (y + k) % ny)
        return remote(src, sets[i][1].at[k - 1, hh], y_s.at[i, k - 1, hh], y_r.at[i, k - 1, hh], y_dev(k))

    def y_send(i):
        for k in range(ny - 1, 0, -1):
            for hh in (0, 1):
                y_copy(i, k, hh).start()

    def y_total(i, hh):
        total = owner_rows(sets[i][0], hh, y)[...].astype(F32)
        for k in range(1, ny):
            total += sets[i][1][k - 1, hh].astype(F32)
        return total

    def h_copy(i):
        return remote(sets[i][2], sets[i][3], xh_s.at[i], xh_r.at[i], h_dev)

    def h_send(i):
        for k in range(1, ny):
            for hh in (0, 1):
                y_copy(i, k, hh).wait_recv()
        sets[i][2][...] = y_total(i, 1 - h).astype(BF16)
        h_copy(i).start()

    def h_last(i):
        total = y_total(i, h)
        h_copy(i).wait_recv()
        sets[i][4][...] = total + sets[i][3][...].astype(F32)

    for k in range(nz):
        for way in (0, 1):
            rs_q(way, k).start()
    for way in (0, 1):
        for chain in (1, 0):
            rs_z(way, chain, 0).start()
    for k in range(nz):
        for way in (0, 1):
            ag_q(way, k, 1 - x).wait_recv()
    g_block = gall[:, feat(jown)]
    pick(lambda lo, n: nt(g_block, bv[lo : lo + n, :]), 1)
    ar_first(1)
    for way in (0, 1):
        slab(part, zwrap(z - sign(way)), x, way, qcols)[...] = rs_sum(way, 2, 0).astype(BF16)
        rs_z(way, 2, 0).start()
    grads(sp_t, gall[:, feat(jown)], gb_part)
    y_send(0)
    ar_second(1)
    for s in range(1, nz - 1):
        rs_step(s)
        if s == 1:
            hg_some(2)
            ar_third(1)
        if s == min(2, nz - 2):
            ar_last(1, bk_nat, bk_t)
            grads(bk_t, hk[:, unit(c)], ga_part)
            y_send(1)
        if s > 2:
            hg_some(2)
        if s == min(4, nz - 2):
            h_send(0)
    hg_some(len(pieces))
    last = nz - 1
    for way in (0, 1):
        slab(part, z, 1 - x, way, pcols)[...] = rs_sum(way, 1, last).astype(BF16)
        rs_p(way).start()
    for way in (0, 1):
        stage[way, :, qcols] = rs_sum(way, 2, last).astype(BF16)
    h_send(1)
    for way in (0, 1):
        total = rs_sum(way, 0, last)
        rs_p(way).wait_recv()
        stage[way, :, pcols] = (total + xr_p[way].astype(F32)).astype(BF16)
    mix_copy = remote(stage.at[1 - c], mixbuf.at[c], mix_s, mix_r, core_dev)
    mix_copy.start()
    hg_send_copy().wait_recv()
    hg_out[...] = (hg_own[...] + hg_recv[...].astype(F32) + SCALE * nt(bk_nat[...], av[...])).astype(BF16)
    h_last(0)
    h_last(1)
    mixed_out[c] = stage[c]
    remote(stage.at[c], mixbuf.at[1 - c], mix_s, mix_r, core_dev).wait_recv()
    mixed_out[1 - c] = mixbuf[1 - c]

    for i in range(3):
        swap_wait(i)[1].wait_send()
    for way in (0, 1):
        ag_p(way, x).wait_send()
        rs_p(way).wait_send()
        for k in range(nz):
            ag_q(way, k, x).wait_send()
            rs_q(way, k).wait_send()
        for chain in range(3):
            for s in range(nz - 1):
                ag_z(way, chain, s).wait_send()
                rs_z(way, chain, s).wait_send()
    for i in range(2):
        for k in (1, 2, 3):
            arq(i, k).wait_send()
            arf(i, k).wait_send()
        for k in range(1, nz):
            arz(i, k).wait_send()
        for k in range(1, ny):
            for hh in (0, 1):
                y_copy(i, k, hh).wait_send()
        h_copy(i).wait_send()
    hg_send_copy().wait_send()
    mix_copy.wait_send()


def solution(mesh):
    def body(hidden, down_weight, first, second, grad, labels, owned):
        sz = sizes_of(mesh, hidden, grad)
        nz, ny, nb, fb, fh = sz["nz"], sz["ny"], sz["blocks"], sz["block"], sz["half"]
        rows, tokens, units = sz["rows"], sz["tokens"], sz["units"]
        quarter, own_rows = tokens // 4, WIDE // sz["ndp"]
        pw = sz["early"] * fb
        qw = fh - pw
        dma = pltpu.SemaphoreType.DMA
        vmem = pltpu.VMEM
        hop, kk = nz - 1, max(ny - 1, 1)
        scratch = [
            vmem((2 * units, fh), BF16),
            vmem((tokens, 2 * units), BF16),
            vmem((units, WIDE), BF16),
            vmem((WIDE, fb), BF16),
            vmem((tokens, fh), BF16),
            vmem((tokens, fh), BF16),
            vmem((2, hop, 2, rows, pw), BF16),
            vmem((2, hop, rows, qw), BF16),
            vmem((nz, 2, rows, qw), BF16),
            vmem((2, rows, pw), BF16),
            vmem((2, rows, fh), BF16),
            vmem((2, rows, fh), BF16),
            vmem((2, 4, RANK, quarter), F32),
            vmem((2, 4, RANK, quarter), F32),
            vmem((2, nz, RANK, quarter), F32),
            vmem((2, 4, RANK, quarter), F32),
            vmem((tokens, WIDE), BF16),
            vmem((WIDE, tokens), BF16),
            vmem((tokens, WIDE), BF16),
            vmem((WIDE, tokens), BF16),
            vmem((tokens, fb), F32),
            vmem((tokens, units), F32),
            vmem((tokens, units), BF16),
            vmem((tokens, units), BF16),
            vmem((WIDE, fb), BF16),
            vmem((WIDE, units), BF16),
            vmem((kk, 2, own_rows, fb), BF16),
            vmem((kk, 2, own_rows, units), BF16),
            vmem((own_rows, fb), BF16),
            vmem((own_rows, units), BF16),
            vmem((own_rows, fb), BF16),
            vmem((own_rows, units), BF16),
            dma((5,)), dma((3,)), dma((3,)),
            dma((2, 3, hop)), dma((2, 3, hop)), dma((2,)), dma((2,)), dma((2, nz)), dma((2, nz)),
            dma((2, 3, hop)), dma((2, 3, hop)), dma((2, nz)), dma((2, nz)), dma((2,)), dma((2,)), dma, dma,
            dma((2, 3)), dma((2, 3)), dma((2, hop)), dma((2, hop)), dma((2, 3)), dma((2, 3)),
            dma((2, kk, 2)), dma((2, kk, 2)), dma((2,)), dma((2,)), dma, dma,
        ]
        anywhere = pl.BlockSpec(memory_space=pl.ANY)
        on_chip = pl.BlockSpec(memory_space=pltpu.VMEM)
        mixed, hg, ga, gb = pl.pallas_call(
            functools.partial(kernel, sz),
            out_shape=(
                jax.ShapeDtypeStruct((2, rows, fh), BF16),
                jax.ShapeDtypeStruct((tokens, units), BF16),
                jax.ShapeDtypeStruct((own_rows, units), F32),
                jax.ShapeDtypeStruct((own_rows, fb), F32),
            ),
            in_specs=[anywhere] * 5 + [on_chip] * 2 + [pl.BlockSpec(memory_space=pltpu.SMEM)],
            out_specs=(on_chip,) * 4,
            scratch_shapes=scratch,
            compiler_params=pltpu.CompilerParams(
                collective_id=0, has_side_effects=True, vmem_limit_bytes=56 * 1024 * 1024
            ),
        )(hidden, down_weight, first, second, grad, labels.reshape(-1, 1), labels.reshape(1, -1), owned)
        mixed = mixed.reshape(2, rows, nb, fb).transpose(1, 2, 0, 3).reshape(rows, 2 * fh)
        slots = own_rows // RANK
        return mixed, hg, ga.reshape(slots, RANK, units), gb.reshape(slots, RANK, fb)

    in_specs = (
        P("dp", "tensor"),
        P("tensor", None),
        P("tensor", None),
        P(None, "tensor"),
        P(("dp", "tensor"), None),
        P("dp", None),
        P(),
    )
    out_specs = (
        P(("dp", "tensor"), None),
        P("dp", "tensor"),
        P("dp", None, "tensor"),
        P("dp", None, "tensor"),
    )
    return jax.shard_map(body, mesh=mesh, in_specs=in_specs, out_specs=out_specs, check_vma=False)
```

time: 458 us -> 121 us (0.26)
  waiting for transfers between devices: 279 us -> 0 us
  Pallas kernels: 0 us -> 110 us
  blocking collectives: 102 us -> 0 us
  matrix products: 34.6 us -> 0 us
  between operations: 13.9 us -> 0.66 us
  starting transfers between devices: 12.1 us -> 0 us
  other arithmetic: 6.66 us -> 0 us
    reduce_scatter x3 -> x0, waiting for transfers between devices: 211 us -> none  [the longest x1 84.2 us: body(): lax.psum_scatter(ordered_a, 'dp', scatter_dimension=0, tiled=True)]
    pallas_call x0 -> x1, Pallas kernels: none -> 110 us  [body(): pl.pallas_call(functools.partial(kernel, sz), out_shape=(jax.ShapeDtypeSt...]
    psum x1 -> x0, blocking collectives: 102 us -> none  [body(): lax.psum((rank_reduce_share, input_gradient_share), 'tensor')]
    all_gather x1 -> x0, waiting for transfers between devices: 59.6 us -> none  [body(): gathered = lax.all_gather(output_gradient, 'tensor', axis=0, tiled=True)]
    dot_general x8 -> x0, matrix products: 34.6 us -> none  [the longest x5 17.4 us: contract_matrices(): lax.dot_general(left, right, (((left_dim,), (right_dim,)), ((), ())), pre...]
    all_to_all x1 -> x0, starting transfers between devices: 12 us -> none  [body(): lax.all_to_all(rank_expand, 'tensor', split_axis=0, concat_axis=1, tiled=...]
    all_to_all x1 -> x0, waiting for transfers between devices: 8.5 us -> none  [body(): lax.all_to_all(rank_expand, 'tensor', split_axis=0, concat_axis=1, tiled=...]
    gather x2 -> x0, local copies, waits for them, and re-layouts: 5.18 us -> none  [the longest x1 2.9 us: body(): jnp.take(resident_second_factor.reshape(LANGUAGE_COUNT, ADAPTER_RANK, -1)...]
  transfers between devices with their start and end apart: 5 -> 0, of which waited for: 5 -> 0; matrix products, arithmetic and copies ran while one was open for 10% -> 0% of each run, Pallas kernels for 0% -> 0%
where the time goes in v1:
time: 121 us; the launch traced here: 120 us
  Pallas kernels  110 us (91%)
  local copies, waits for them, and re-layouts  8.81 us (7%)
    pallas_call x1, Pallas kernels, body(): pl.pallas_call(functools.partial(kernel, sz), out_shape=(jax.ShapeDtypeSt...  110 us
    unnamed x4, local copies, waits for them, and re-layouts  6.1 us

profile of v1, /device:TPU:32, one launch (start us, length us, event | category | flops | bytes accessed | tf_op | source)
XLA Modules:
  0.0 120.0 jit_solution(16316902295842245565)
XLA Ops:
  0.6 1.5 %copy.12.lab_col = s32[512,1]{1,0:T(8,128)} copy(s32[512,1]{0,1:T(1,128)} %bitcast.15) | data formatting | bytes 4096 | tf_op jit(solution)/shard_map/reshape | solution.py:565
  2.2 110.5 %shard_map.102 = (bf16[2,16,4096]{2,1,0:T(8,128)(2,1)}, bf16[512,512]{1,0:T(8,128)(2,1)}, f32[128,512]{1,0:T(8,128)}, f32[128,256]{1,0:T(8,128)}) custom-call(bf16[512,512]{1,0:T(8,128)(2,1)} %hidden_ref.1, bf16[512,8192]{1,0:T(8,128)(2,1)} %weight_ref.1, bf16[512,1024]{1,0:T(8,128)(2,1)} %first_ref.1, bf16[1024,256]{1,0:T(8,128)(2,1)} %second_ref.1, ...), custom_call_target="tpu_custom_call" | custom-call | tf_op jit(solution)/shard_map/pallas_call | solution.py:551
  112.7 1.0 copy.14
  113.7 0.3 copy.13
  114.0 0.9 reshape.25
  114.9 1.9 %copy.18 = bf16[512,512]{1,0:T(8,128)(2,1)} copy(bf16[512,512]{1,0:T(8,128)(2,1)} %get-tuple-element.17) | data formatting | bytes 1048576
  116.7 1.7 %copy.19 = f32[8,16,512]{2,1,0:T(8,128)} copy(f32[8,16,512]{2,1,0:T(8,128)} %bitcast.12) | data formatting | bytes 524288
  118.4 1.6 %copy.20 = f32[8,16,256]{2,1,0:T(8,128)} copy(f32[8,16,256]{2,1,0:T(8,128)} %bitcast.14) | data formatting | bytes 262144
  (1 shorter events, 0.0 us)

commit v2 on v1

--- a/solution.py
+++ b/solution.py
@@ -44,10 +44,10 @@
 
 def kernel(
     sz,
-    hidden_ref, weight_ref, first_ref, second_ref, grad_ref, lab_col, lab_row, own_ref,
+    hidden_ref, weight_ref, first_ref, second_ref, grad_ref, lab_row, own_ref,
     mixed_out, hg_out, ga_out, gb_out,
     wk, hk, av, bv, gall, part, zr_p, zr_q, xr_q, xr_p, stage, mixbuf,
-    ar_own, ar_quad, ar_z, ar_fin, sp_nat, sp_t, bk_nat, bk_t, lift,
+    lab_col, ar_own, ar_quad, ar_z, ar_fin, sp_nat, sp_t, bk_nat, bk_t, lift,
     hg_own, hg_send, hg_recv, gb_part, ga_part, yr_b, yr_a, xs_b, xs_a, xr_b, xr_a,
     load_sem, swap_send, swap_recv,
     agz_s, agz_r, agp_s, agp_r, agq_s, agq_r,
@@ -118,6 +118,7 @@
     load_b = pltpu.make_async_copy(second_ref, bv, load_sem.at[3])
     load_h.start()
     load_a.start()
+    lab_col[...] = jnp.broadcast_to(lab_row[...], (LANES, tokens)).T
     pl.semaphore_wait(barrier, len(peers))
 
     for j in range(nb):
@@ -199,7 +200,7 @@
     per = LANES // RANK
 
     def pick(product, i):
-        labels = jnp.broadcast_to(lab_col[...], (tokens, LANES))
+        labels = lab_col[...]
         total = jnp.zeros((tokens, LANES), F32)
         step = 2 * LANES
         for g in range(WIDE // step):
@@ -269,7 +270,7 @@
         for k in range(LANGS):
             turned[k * RANK : (k + 1) * RANK, :] = jnp.where(languages == own_ref[k], small, 0.0).astype(BF16)
         tall = jnp.concatenate([small] * per, axis=0).T
-        labels = jnp.broadcast_to(lab_col[...], (tokens, LANES))
+        labels = lab_col[...]
         for g in range(WIDE // LANES):
             natural[:, g * LANES : (g + 1) * LANES] = jnp.where(
                 labels == lane_lang + g * per, tall, 0.0
@@ -293,23 +294,6 @@
     h_own = hk[:, unit(c)]
     pick(lambda lo, n: nn(h_own, av[:, lo : lo + n]), 0)
     ar_first(0)
-
-    splits = [(nb - 1) * s // (nz - 1) for s in range(nz)]
-    for s in range(nz - 1):
-        ag_step(s)
-        if s == 0:
-            ar_second(0)
-            swap_wait(1)[0].wait_recv()
-            swap_wait(2)[0].wait_recv()
-            pltpu.make_async_copy(wk.at[unit(c), :], wk.at[unit(c), :], load_sem.at[4]).wait()
-        if s == min(2, nz - 2):
-            ar_third(0)
-        if s == min(3, nz - 2):
-            load_b.wait()
-            ar_last(0, sp_nat, sp_t)
-            lift[...] = SCALE * nn(sp_nat[...], bv[...])
-        mix_blocks(splits[s], splits[s + 1])
-    mix_own()
 
     def rs_z(way, chain, s):
         src = slab(part, zwrap(z - sign(way) * (s + 1)), chain_x(chain), way, chain_cols[chain])
@@ -337,13 +321,52 @@
             total += got.astype(F32)
         return total
 
+    def rs_ahead(k):
+        if k < nz:
+            for way in (0, 1):
+                rs_q(way, k).start()
+
     def rs_step(s):
+        rs_ahead(s + 2)
         for chain in (1, 2, 0):
             for way in (0, 1):
                 if s > 0 or chain == 2:
                     zs = zwrap(z - sign(way) * (s + 1))
                     slab(part, zs, chain_x(chain), way, chain_cols[chain])[...] = rs_sum(way, chain, s).astype(BF16)
                 rs_z(way, chain, s).start()
+
+    first_mix = min(1, nz - 2)
+    last_mix = max(nz - 3, first_mix)
+    spans = last_mix - first_mix + 1
+    splits = [(nb - 1) * n // spans for n in range(spans + 1)]
+
+    def shrink_done():
+        ar_last(0, sp_nat, sp_t)
+        lift[...] = SCALE * nn(sp_nat[...], bv[...])
+
+    for s in range(nz - 2):
+        ag_step(s)
+        if s == 0:
+            ar_second(0)
+        if s == first_mix:
+            swap_wait(1)[0].wait_recv()
+            swap_wait(2)[0].wait_recv()
+            pltpu.make_async_copy(wk.at[unit(c), :], wk.at[unit(c), :], load_sem.at[4]).wait()
+            load_b.wait()
+        if s == min(3, last_mix):
+            ar_third(0)
+        if s == last_mix:
+            shrink_done()
+        if s >= first_mix:
+            mix_blocks(splits[s - first_mix], splits[s - first_mix + 1])
+    mix_own()
+    for way in (0, 1):
+        for chain in (1, 0):
+            rs_z(way, chain, 0).start()
+    ag_step(nz - 2)
+    for k in (0, 1):
+        for way in (0, 1):
+            rs_q(way, k).start()
 
     tile = min(256, units)
     mtile = tokens // 2
@@ -387,18 +410,33 @@
     def owner_rows(ref, hh, yy):
         return ref.at[pl.ds(aligned((hh * ny + yy) * own_rows, own_rows), own_rows), :]
 
+    def y_hop(k, hh):
+        return k if k in (1, ny - 1) else (ny - 1 if hh else 1)
+
+    relayed = ((1, 0), (3, 1)) if ny == 4 else ()
+
     def y_copy(i, k, hh):
         src = owner_rows(sets[i][0], hh, (y + k) % ny)
-        return remote(src, sets[i][1].at[k - 1, hh], y_s.at[i, k - 1, hh], y_r.at[i, k - 1, hh], y_dev(k))
+        return remote(src, sets[i][1].at[k - 1, hh], y_s.at[i, k - 1, hh], y_r.at[i, k - 1, hh], y_dev(y_hop(k, hh)))
 
     def y_send(i):
-        for k in range(ny - 1, 0, -1):
+        for k in (2, 1, 3) if ny == 4 else range(1, ny):
             for hh in (0, 1):
-                y_copy(i, k, hh).start()
+                if (k, hh) not in relayed:
+                    y_copy(i, k, hh).start()
+
+    def y_mid(i):
+        for k, hh in relayed:
+            y_copy(i, 2, hh).wait_recv()
+            mine = owner_rows(sets[i][0], hh, (y + k) % ny)
+            mine[...] = (mine[...].astype(F32) + sets[i][1][1, hh].astype(F32)).astype(BF16)
+            y_copy(i, k, hh).start()
+
+    y_direct = (1, 3) if ny == 4 else tuple(range(1, ny))
 
     def y_total(i, hh):
         total = owner_rows(sets[i][0], hh, y)[...].astype(F32)
-        for k in range(1, ny):
+        for k in y_direct:
             total += sets[i][1][k - 1, hh].astype(F32)
         return total
 
@@ -406,7 +444,7 @@
         return remote(sets[i][2], sets[i][3], xh_s.at[i], xh_r.at[i], h_dev)
 
     def h_send(i):
-        for k in range(1, ny):
+        for k in y_direct:
             for hh in (0, 1):
                 y_copy(i, k, hh).wait_recv()
         sets[i][2][...] = y_total(i, 1 - h).astype(BF16)
@@ -417,12 +455,6 @@
         h_copy(i).wait_recv()
         sets[i][4][...] = total + sets[i][3][...].astype(F32)
 
-    for k in range(nz):
-        for way in (0, 1):
-            rs_q(way, k).start()
-    for way in (0, 1):
-        for chain in (1, 0):
-            rs_z(way, chain, 0).start()
     for k in range(nz):
         for way in (0, 1):
             ag_q(way, k, 1 - x).wait_recv()
@@ -432,22 +464,28 @@
     for way in (0, 1):
         slab(part, zwrap(z - sign(way)), x, way, qcols)[...] = rs_sum(way, 2, 0).astype(BF16)
         rs_z(way, 2, 0).start()
+    rs_ahead(2)
     grads(sp_t, gall[:, feat(jown)], gb_part)
     y_send(0)
-    ar_second(1)
+    at = {name: min(s, nz - 2) for name, s in dict(second=1, mid_b=2, third=3, back=4, h_b=5, mid_a=6).items()}
     for s in range(1, nz - 1):
         rs_step(s)
-        if s == 1:
-            hg_some(2)
+        if s == at["second"]:
+            ar_second(1)
+        if s == at["mid_b"]:
+            y_mid(0)
+        if s == at["third"]:
             ar_third(1)
-        if s == min(2, nz - 2):
+        if s == at["back"]:
             ar_last(1, bk_nat, bk_t)
             grads(bk_t, hk[:, unit(c)], ga_part)
             y_send(1)
-        if s > 2:
+        else:
             hg_some(2)
-        if s == min(4, nz - 2):
+        if s == at["h_b"]:
             h_send(0)
+        if s == at["mid_a"]:
+            y_mid(1)
     hg_some(len(pieces))
     last = nz - 1
     for way in (0, 1):
@@ -466,9 +504,11 @@
     hg_out[...] = (hg_own[...] + hg_recv[...].astype(F32) + SCALE * nt(bk_nat[...], av[...])).astype(BF16)
     h_last(0)
     h_last(1)
-    mixed_out[c] = stage[c]
+    for j in range(nb):
+        mixed_out[:, feat(2 * j + c)] = stage[c, :, j * fb : (j + 1) * fb]
     remote(stage.at[c], mixbuf.at[1 - c], mix_s, mix_r, core_dev).wait_recv()
-    mixed_out[1 - c] = mixbuf[1 - c]
+    for j in range(nb):
+        mixed_out[:, feat(2 * j + 1 - c)] = mixbuf[1 - c, :, j * fb : (j + 1) * fb]
 
     for i in range(3):
         swap_wait(i)[1].wait_send()
@@ -520,6 +560,7 @@
             vmem((2, rows, pw), BF16),
             vmem((2, rows, fh), BF16),
             vmem((2, rows, fh), BF16),
+            vmem((tokens, LANES), jnp.int32),
             vmem((2, 4, RANK, quarter), F32),
             vmem((2, 4, RANK, quarter), F32),
             vmem((2, nz, RANK, quarter), F32),
@@ -551,19 +592,18 @@
         mixed, hg, ga, gb = pl.pallas_call(
             functools.partial(kernel, sz),
             out_shape=(
-                jax.ShapeDtypeStruct((2, rows, fh), BF16),
+                jax.ShapeDtypeStruct((rows, 2 * fh), BF16),
                 jax.ShapeDtypeStruct((tokens, units), BF16),
                 jax.ShapeDtypeStruct((own_rows, units), F32),
                 jax.ShapeDtypeStruct((own_rows, fb), F32),
             ),
-            in_specs=[anywhere] * 5 + [on_chip] * 2 + [pl.BlockSpec(memory_space=pltpu.SMEM)],
+            in_specs=[anywhere] * 5 + [on_chip] + [pl.BlockSpec(memory_space=pltpu.SMEM)],
             out_specs=(on_chip,) * 4,
             scratch_shapes=scratch,
             compiler_params=pltpu.CompilerParams(
                 collective_id=0, has_side_effects=True, vmem_limit_bytes=56 * 1024 * 1024
             ),
-        )(hidden, down_weight, first, second, grad, labels.reshape(-1, 1), labels.reshape(1, -1), owned)
-        mixed = mixed.reshape(2, rows, nb, fb).transpose(1, 2, 0, 3).reshape(rows, 2 * fh)
+        )(hidden, down_weight, first, second, grad, labels, owned)
         slots = own_rows // RANK
         return mixed, hg, ga.reshape(slots, RANK, units), gb.reshape(slots, RANK, fb)
 

time: 121 us -> 102 us (0.84)
  Pallas kernels: 110 us -> 94.5 us
  local copies, waits for them, and re-layouts: 8.81 us -> 6.77 us
    pallas_call x1, Pallas kernels: 110 us -> 94.5 us  [body(): pl.pallas_call(functools.partial(kernel, sz), out_shape=(jax.ShapeDtypeSt...]
    reshape x2 -> x0, local copies, waits for them, and re-layouts: 2.42 us -> none  [the longest x1 1.54 us: body(): labels.reshape(-1, 1)]
where the time goes in v2:
time: 102 us
  Pallas kernels  94.5 us (93%)
  local copies, waits for them, and re-layouts  6.77 us (7%)
    pallas_call x1, Pallas kernels, body(): pl.pallas_call(functools.partial(kernel, sz), out_shape=(jax.ShapeDtypeSt...  94.5 us
    unnamed x4, local copies, waits for them, and re-layouts  6.77 us

profile of v2, /device:TPU:32, one launch (start us, length us, event | category | flops | bytes accessed | tf_op | source)
XLA Modules:
  0.0 102.0 jit_solution(2828507184685056326)
XLA Ops:
  0.6 94.5 %shard_map.102 = (bf16[16,8192]{1,0:T(8,128)(2,1)}, bf16[512,512]{1,0:T(8,128)(2,1)}, f32[128,512]{1,0:T(8,128)}, f32[128,256]{1,0:T(8,128)}) custom-call(bf16[512,512]{1,0:T(8,128)(2,1)} %hidden_ref.1, bf16[512,8192]{1,0:T(8,128)(2,1)} %weight_ref.1, bf16[512,1024]{1,0:T(8,128)(2,1)} %first_ref.1, bf16[1024,256]{1,0:T(8,128)(2,1)} %second_ref.1, ...), custom_call_target="tpu_custom_call" | custom-call | tf_op jit(solution)/shard_map/pallas_call | solution.py:592
  95.2 1.7 %copy.15 = bf16[16,8192]{1,0:T(8,128)(2,1)} copy(bf16[16,8192]{1,0:T(8,128)(2,1)} %get-tuple-element.16) | data formatting | bytes 524288
  96.9 1.9 %copy.16 = bf16[512,512]{1,0:T(8,128)(2,1)} copy(bf16[512,512]{1,0:T(8,128)(2,1)} %get-tuple-element.17) | data formatting | bytes 1048576
  98.7 1.7 %copy.17 = f32[8,16,512]{2,1,0:T(8,128)} copy(f32[8,16,512]{2,1,0:T(8,128)} %bitcast.2) | data formatting | bytes 524288
  100.4 1.6 %copy.18 = f32[8,16,256]{2,1,0:T(8,128)} copy(f32[8,16,256]{2,1,0:T(8,128)} %bitcast.3) | data formatting | bytes 262144

commit v3 on v2

--- a/solution.py
+++ b/solution.py
@@ -38,7 +38,7 @@
         rows=grad.shape[0],
         tokens=hidden.shape[0],
         units=hidden.shape[1],
-        early=blocks * 7 // 16,
+        early=blocks * 6 // 16,
     )
 
 
@@ -176,8 +176,9 @@
     pltpu.make_async_copy(
         slab(gall, z, x, c, whole), slab(gall, z, x, c, whole), load_sem.at[0]
     ).wait()
-    swap_wait(0)[0].wait_recv()
-    for way in (0, 1):
+    for way in (c, 1 - c):
+        if way is not c:
+            swap_wait(0)[0].wait_recv()
         ag_p(way, x).start()
         ag_z(way, 0, 0).start()
         ag_z(way, 2, 0).start()
@@ -487,6 +488,8 @@
         if s == at["mid_a"]:
             y_mid(1)
     hg_some(len(pieces))
+    hg_send_copy().wait_recv()
+    hg_out[...] = (hg_own[...] + hg_recv[...].astype(F32) + SCALE * nt(bk_nat[...], av[...])).astype(BF16)
     last = nz - 1
     for way in (0, 1):
         slab(part, z, 1 - x, way, pcols)[...] = rs_sum(way, 1, last).astype(BF16)
@@ -500,8 +503,6 @@
         stage[way, :, pcols] = (total + xr_p[way].astype(F32)).astype(BF16)
     mix_copy = remote(stage.at[1 - c], mixbuf.at[c], mix_s, mix_r, core_dev)
     mix_copy.start()
-    hg_send_copy().wait_recv()
-    hg_out[...] = (hg_own[...] + hg_recv[...].astype(F32) + SCALE * nt(bk_nat[...], av[...])).astype(BF16)
     h_last(0)
     h_last(1)
     for j in range(nb):
@@ -534,6 +535,21 @@
         h_copy(i).wait_send()
     hg_send_copy().wait_send()
     mix_copy.wait_send()
+
+
+def deliver(*refs):
+    n = (len(refs) - 2) // 3
+    sources, targets, held = refs[:n], refs[n : 2 * n], refs[2 * n : 3 * n]
+    load, store = refs[3 * n :]
+    ins = [pltpu.make_async_copy(a, v, load.at[i]) for i, (a, v) in enumerate(zip(sources, held))]
+    outs = [pltpu.make_async_copy(v, b, store.at[i]) for i, (v, b) in enumerate(zip(held, targets))]
+    for copy in ins:
+        copy.start()
+    for fetched, stored in zip(ins, outs):
+        fetched.wait()
+        stored.start()
+    for copy in outs:
+        copy.wait()
 
 
 def solution(mesh):
@@ -604,6 +620,15 @@
                 collective_id=0, has_side_effects=True, vmem_limit_bytes=56 * 1024 * 1024
             ),
         )(hidden, down_weight, first, second, grad, labels, owned)
+        results = (mixed, hg, ga, gb)
+        shapes = [jax.ShapeDtypeStruct(r.shape, r.dtype) for r in results]
+        mixed, hg, ga, gb = pl.pallas_call(
+            deliver,
+            out_shape=shapes,
+            in_specs=[anywhere] * 4,
+            out_specs=[anywhere] * 4,
+            scratch_shapes=[vmem(r.shape, r.dtype) for r in results] + [dma((4,)), dma((4,))],
+        )(*results)
         slots = own_rows // RANK
         return mixed, hg, ga.reshape(slots, RANK, units), gb.reshape(slots, RANK, fb)
 

time: 102 us -> 95.8 us (0.939)
  local copies, waits for them, and re-layouts: 6.77 us -> 0 us
    unnamed x4 -> x0, local copies, waits for them, and re-layouts: 6.77 us -> none
    pallas_call x1, Pallas kernels: 94.5 us -> 92.4 us  [body(): pl.pallas_call(functools.partial(kernel, sz), out_shape=(jax.ShapeDtypeSt...]
    pallas_call x0 -> x1, Pallas kernels: none -> 2.11 us  [body(): pl.pallas_call(deliver, out_shape=shapes, in_specs=[anywhere] * 4, out_sp...]
where the time goes in v3:
time: 95.8 us; the launch traced here: 95.3 us
  Pallas kernels  94.5 us (99%)
    pallas_call x1, Pallas kernels, body(): pl.pallas_call(functools.partial(kernel, sz), out_shape=(jax.ShapeDtypeSt...  92.4 us
    pallas_call x1, Pallas kernels, body(): pl.pallas_call(deliver, out_shape=shapes, in_specs=[anywhere] * 4, out_sp...  2.11 us

profile of v3, /device:TPU:32, one launch (start us, length us, event | category | flops | bytes accessed | tf_op | source)
XLA Modules:
  0.0 95.3 jit_solution(4436950866505370969)
XLA Ops:
  0.6 92.4 %shard_map.102 = (bf16[16,8192]{1,0:T(8,128)(2,1)}, bf16[512,512]{1,0:T(8,128)(2,1)}, f32[128,512]{1,0:T(8,128)}, f32[128,256]{1,0:T(8,128)}) custom-call(bf16[512,512]{1,0:T(8,128)(2,1)} %hidden_ref.1, bf16[512,8192]{1,0:T(8,128)(2,1)} %weight_ref.1, bf16[512,1024]{1,0:T(8,128)(2,1)} %first_ref.1, bf16[1024,256]{1,0:T(8,128)(2,1)} %second_ref.1, ...), custom_call_target="tpu_custom_call" | custom-call | tf_op jit(solution)/shard_map/pallas_call | solution.py:608
  93.0 2.1 %shard_map.103 = (bf16[16,8192]{1,0:T(8,128)(2,1)}, bf16[512,512]{1,0:T(8,128)(2,1)}, f32[128,512]{1,0:T(8,128)}, f32[128,256]{1,0:T(8,128)}) custom-call(bf16[16,8192]{1,0:T(8,128)(2,1)} %get-tuple-element.12.refs_0_, bf16[512,512]{1,0:T(8,128)(2,1)} %get-tuple-element.13.refs_1_, f32[128,512]{1,0:T(8,128)} %get-tuple-element.14.refs_2_, ...), custom_call_target="tpu_custom_call" | custom-call | tf_op jit(solution)/shard_map/pallas_call | solution.py:625
